TPU v7x, 32 devices: a whole 2x2x4 slice. The times are simulated.
32 devices in a mesh: dp: 16 (over z, x, core), tensor: 2 (over y).
Axes of the slice: x: 2, y: 2, z: 4, core: 2. Of those that a mesh axis runs over, the one named last changes fastest.
Arguments:
- tokens: bfloat16 [32768, 768], P(('dp', 'tensor')), may hold values from -6 to 6
- segment_ids: int32 [16, 2048], P('dp'), may hold values from 0 to 15, never falling along the last dimension, each value on 1 to 1024 neighbouring positions
- ln1_gain: bfloat16 [768], P('dp'), may hold values from 0.25 to 1.75
- ln1_bias: bfloat16 [768], P('dp'), may hold values from -1.796875 to 1.796875
- w_qkv: bfloat16 [768, 3, 768], P('dp', None, 'tensor'), may hold values from -0.3125 to 0.3125
- b_qv: bfloat16 [2, 768], P(None, 'dp'), may hold values from -1.796875 to 1.796875
- w_attn_out: bfloat16 [768, 768], P('tensor', 'dp'), may hold values from -3 to 3
- b_attn_out: bfloat16 [768], P('dp'), may hold values from -6 to 6
- ln2_gain: bfloat16 [768], P('dp'), may hold values from 0.25 to 1.75
- ln2_bias: bfloat16 [768], P('dp'), may hold values from -1.796875 to 1.796875
- w_fc: bfloat16 [768, 3072], P('dp', 'tensor'), may hold values from -0.21875 to 0.21875
- b_fc: bfloat16 [3072], P('dp'), may hold values from -1.796875 to 1.796875
- w_proj: bfloat16 [3072, 768], P('tensor', 'dp'), may hold values from -0.8984375 to 0.8984375
- b_proj: bfloat16 [768], P('dp'), may hold values from -6 to 6
- cotangent: bfloat16 [32768, 768], P(('dp', 'tensor')), may hold values from -6 to 6
Outputs:
- block_out: bfloat16 [32768, 768], P(('dp', 'tensor'))
- grad_tokens: bfloat16 [32768, 768], P(('dp', 'tensor'))
- grad_ln1_gain: float32 [768], P('dp')
- grad_ln1_bias: float32 [768], P('dp')
- grad_w_qkv: float32 [768, 3, 768], P('dp', None, 'tensor')
- grad_b_qv: float32 [2, 768], P(None, 'dp')
- grad_w_attn_out: float32 [768, 768], P('tensor', 'dp')
- grad_b_attn_out: float32 [768], P('dp')
- grad_ln2_gain: float32 [768], P('dp')
- grad_ln2_bias: float32 [768], P('dp')
- grad_w_fc: float32 [768, 3072], P('dp', 'tensor')
- grad_b_fc: float32 [3072], P('dp')
- grad_w_proj: float32 [3072, 768], P('tensor', 'dp')
- grad_b_proj: float32 [768], P('dp')
Inputs may be any that keep to these rules, and one draw needn't show every extreme that they name: `segment_ids`: in each sequence the document numbers never fall; each document has 1 to 1024 tokens, and one has exactly 1024.
All inputs are finite; a program needn't handle non-finite values.
Results may differ from a plain program's by a relative error of at most 0.02.
Values may be sent and summed in bfloat16 or wider, within the bound.
A program may use at most 256 MiB of HBM per device.

v0:
```python
import jax
import jax.numpy as jnp
from jax import lax
from jax.sharding import PartitionSpec as P

HEAD_DIM = 64
EPSILON = 1e-05
BRANCH_SCALE = 48.0 ** (-0.5)
MASKED_SCORE = -1e30


def layer_norm(values, gain, offsets):
    centered = values - jnp.mean(values, axis=-1, keepdims=True)
    variance = jnp.mean(centered * centered, axis=-1, keepdims=True)
    return centered * lax.rsqrt(variance + EPSILON) * gain + offsets


def gelu_tanh(values):
    return jax.nn.gelu(values, approximate=True)


def contract_rows(left, right):
    return lax.dot_general(
        left, right, (((0,), (0,)), ((), ())), preferred_element_type=jnp.float32
    )


def contract_cols(left, right):
    return lax.dot_general(
        left, right, (((1,), (1,)), ((), ())), preferred_element_type=jnp.float32
    )


def visible_mask(seg_row, row_start, block_rows):
    seq_len = seg_row.shape[0]
    seg_query = lax.dynamic_slice_in_dim(seg_row, row_start, block_rows, 0)
    query_pos = row_start + jnp.arange(block_rows, dtype=jnp.int32)
    key_pos = jnp.arange(seq_len, dtype=jnp.int32)
    return (seg_query[:, None] == seg_row[None, :]) & (query_pos[:, None] >= key_pos[None, :])


def on_device(
    tokens,
    segment_ids,
    ln1_gain,
    ln1_bias,
    w_qkv,
    b_qv,
    w_attn_out,
    b_attn_out,
    ln2_gain,
    ln2_bias,
    w_fc,
    b_fc,
    w_proj,
    b_proj,
    cotangent,
):
    model_width = tokens.shape[1]
    local_rows = tokens.shape[0]
    local_cols = w_qkv.shape[2]
    hidden_cols = w_fc.shape[1]
    heads_here = local_cols // HEAD_DIM
    seg_row = segment_ids[0]
    seq_len = seg_row.shape[0]
    score_scale = HEAD_DIM ** (-0.5)
    tensor_pos = lax.axis_index("tensor")
    gain_attn, offset_attn, qkv_weight, qv_bias_all, out_weight, out_bias = (
        lax.all_gather(ln1_gain, "dp", axis=0, tiled=True),
        lax.all_gather(ln1_bias, "dp", axis=0, tiled=True),
        lax.all_gather(w_qkv, "dp", axis=0, tiled=True),
        lax.all_gather(b_qv, "dp", axis=1, tiled=True),
        lax.all_gather(w_attn_out, "dp", axis=1, tiled=True),
        lax.all_gather(b_attn_out, "dp", axis=0, tiled=True),
    )
    qkv_flat_weight = qkv_weight.reshape(model_width, 3 * local_cols)
    qv_bias = lax.dynamic_slice_in_dim(qv_bias_all, tensor_pos * local_cols, local_cols, 1).astype(
        jnp.float32
    )
    qkv_bias = jnp.stack([qv_bias[0], jnp.zeros((local_cols,), jnp.float32), qv_bias[1]])
    residual_in = tokens.astype(jnp.float32)
    normed_one = layer_norm(
        residual_in, gain_attn.astype(jnp.float32), offset_attn.astype(jnp.float32)
    ).astype(jnp.bfloat16)
    full_one = lax.all_gather(normed_one, "tensor", axis=0, tiled=True)
    projected = (
        jnp.dot(full_one, qkv_flat_weight, preferred_element_type=jnp.float32).reshape(
            seq_len, 3, local_cols
        )
        + qkv_bias
    ).astype(jnp.bfloat16)
    queries = projected[:, 0]
    keys_all = projected[:, 1]
    values_all = projected[:, 2]
    block_rows = min(512, seq_len)
    starts = jnp.arange(seq_len // block_rows, dtype=jnp.int32) * block_rows

    def forward_block(row_start):
        visible = visible_mask(seg_row, row_start, block_rows)
        query_block = lax.dynamic_slice_in_dim(queries, row_start, block_rows, 0)
        pieces = []
        logsums = []
        for head_index in range(heads_here):
            low_col = head_index * HEAD_DIM
            high_col = low_col + HEAD_DIM
            raw_scores = contract_cols(
                query_block[:, low_col:high_col], keys_all[:, low_col:high_col]
            )
            scores = jnp.where(visible, raw_scores * score_scale, MASKED_SCORE)
            row_max = jnp.max(scores, axis=1, keepdims=True)
            exponent = jnp.exp(scores - row_max)
            row_total = jnp.sum(exponent, axis=1, keepdims=True)
            soft_weights = (exponent / row_total).astype(jnp.bfloat16)
            pieces.append(
                jnp.dot(
                    soft_weights,
                    values_all[:, low_col:high_col],
                    preferred_element_type=jnp.float32,
                )
            )
            logsums.append(row_max[:, 0] + jnp.log(row_total[:, 0]))
        return (jnp.concatenate(pieces, axis=1).astype(jnp.bfloat16), jnp.stack(logsums))

    attn_blocks, logsum_blocks = lax.map(forward_block, starts)
    attended = attn_blocks.reshape(seq_len, local_cols)
    attn_branch = lax.psum_scatter(
        jnp.dot(
            lax.slice_in_dim(attended, 0, lax.axis_size("tensor") * local_rows, axis=0),
            out_weight,
            preferred_element_type=jnp.float32,
        ).astype(jnp.bfloat16),
        "tensor",
        scatter_dimension=0,
        tiled=True,
    ).astype(jnp.float32) + out_bias.astype(jnp.float32)
    middle = residual_in + BRANCH_SCALE * attn_branch
    gain_mlp, offset_mlp, fc_weight, fc_bias_all, proj_weight, proj_bias = (
        lax.all_gather(ln2_gain, "dp", axis=0, tiled=True),
        lax.all_gather(ln2_bias, "dp", axis=0, tiled=True),
        lax.all_gather(w_fc, "dp", axis=0, tiled=True),
        lax.all_gather(b_fc, "dp", axis=0, tiled=True),
        lax.all_gather(w_proj, "dp", axis=1, tiled=True),
        lax.all_gather(b_proj, "dp", axis=0, tiled=True),
    )
    fc_bias = lax.dynamic_slice_in_dim(
        fc_bias_all, tensor_pos * hidden_cols, hidden_cols, 0
    ).astype(jnp.float32)
    normed_two = layer_norm(
        middle, gain_mlp.astype(jnp.float32), offset_mlp.astype(jnp.float32)
    ).astype(jnp.bfloat16)
    full_two = lax.all_gather(normed_two, "tensor", axis=0, tiled=True)
    inputs_rows = lax.slice_in_dim(full_two, 0, lax.axis_size("tensor") * local_rows, axis=0)
    activated = gelu_tanh(
        jnp.dot(inputs_rows, fc_weight, preferred_element_type=jnp.float32) + fc_bias
    ).astype(jnp.bfloat16)
    mlp_branch = lax.psum_scatter(
        jnp.dot(activated, proj_weight, preferred_element_type=jnp.float32).astype(jnp.bfloat16),
        "tensor",
        scatter_dimension=0,
        tiled=True,
    ).astype(jnp.float32) + proj_bias.astype(jnp.float32)
    block_out = (middle + BRANCH_SCALE * mlp_branch).astype(jnp.bfloat16)
    (
        gain_attn,
        offset_attn,
        qkv_weight,
        out_weight,
        gain_mlp,
        offset_mlp,
        fc_weight,
        fc_bias_all,
        proj_weight,
    ) = (
        lax.all_gather(ln1_gain, "dp", axis=0, tiled=True),
        lax.all_gather(ln1_bias, "dp", axis=0, tiled=True),
        lax.all_gather(w_qkv, "dp", axis=0, tiled=True),
        lax.all_gather(w_attn_out, "dp", axis=1, tiled=True),
        lax.all_gather(ln2_gain, "dp", axis=0, tiled=True),
        lax.all_gather(ln2_bias, "dp", axis=0, tiled=True),
        lax.all_gather(w_fc, "dp", axis=0, tiled=True),
        lax.all_gather(b_fc, "dp", axis=0, tiled=True),
        lax.all_gather(w_proj, "dp", axis=1, tiled=True),
    )
    qkv_flat_weight = qkv_weight.reshape(model_width, 3 * local_cols)
    fc_bias = lax.dynamic_slice_in_dim(
        fc_bias_all, tensor_pos * hidden_cols, hidden_cols, 0
    ).astype(jnp.float32)
    grad_out = cotangent.astype(jnp.float32)
    scaled_out = BRANCH_SCALE * grad_out
    d_proj_bias = jnp.sum(scaled_out, axis=0)
    d_mlp_full = lax.all_gather(scaled_out.astype(jnp.bfloat16), "tensor", axis=0, tiled=True)
    mlp_block = min(1024, seq_len)

    def mlp_back_block(row_start):
        inputs_rows = lax.dynamic_slice_in_dim(full_two, row_start, mlp_block, 0)
        grad_rows = lax.dynamic_slice_in_dim(d_mlp_full, row_start, mlp_block, 0)
        pre_act = jnp.dot(inputs_rows, fc_weight, preferred_element_type=jnp.float32) + fc_bias
        activated, gelu_back = jax.vjp(gelu_tanh, pre_act)
        d_act = contract_cols(grad_rows, proj_weight)
        d_pre = gelu_back(d_act)[0]
        return (activated.astype(jnp.bfloat16), d_pre.astype(jnp.bfloat16), jnp.sum(d_pre, axis=0))

    act_blocks, dpre_blocks, dbias_blocks = lax.map(
        mlp_back_block, jnp.arange(seq_len // mlp_block, dtype=jnp.int32) * mlp_block
    )
    act_all = act_blocks.reshape(seq_len, hidden_cols)
    d_pre_all = dpre_blocks.reshape(seq_len, hidden_cols)
    d_fc_bias = jnp.sum(dbias_blocks, axis=0)
    d_proj_w = contract_rows(act_all, d_mlp_full)
    d_fc_w = contract_rows(full_two, d_pre_all)
    grad_w_fc, grad_w_proj = (
        lax.psum_scatter(d_fc_w, "dp", scatter_dimension=0, tiled=True),
        lax.psum_scatter(d_proj_w, "dp", scatter_dimension=1, tiled=True),
    )
    d_normed_two = lax.psum_scatter(
        contract_cols(
            lax.slice_in_dim(d_pre_all, 0, lax.axis_size("tensor") * local_rows, axis=0), fc_weight
        ).astype(jnp.bfloat16),
        "tensor",
        scatter_dimension=0,
        tiled=True,
    ).astype(jnp.float32)
    unused_two, norm_back_two = jax.vjp(
        layer_norm, middle, gain_mlp.astype(jnp.float32), offset_mlp.astype(jnp.float32)
    )
    d_middle_part, d_gain_mlp, d_offset_mlp = norm_back_two(d_normed_two)
    d_middle = grad_out + d_middle_part
    scaled_mid = BRANCH_SCALE * d_middle
    d_out_bias = jnp.sum(scaled_mid, axis=0)
    d_attn_full = lax.all_gather(scaled_mid.astype(jnp.bfloat16), "tensor", axis=0, tiled=True)
    d_out_w = contract_rows(attended, d_attn_full)
    d_attended = contract_cols(d_attn_full, out_weight).astype(jnp.bfloat16)

    def backward_block(carry, inputs):
        d_keys_acc, d_values_acc = carry
        row_start, logsum = inputs
        visible = visible_mask(seg_row, row_start, block_rows)
        query_block = lax.dynamic_slice_in_dim(queries, row_start, block_rows, 0)
        grad_block = lax.dynamic_slice_in_dim(d_attended, row_start, block_rows, 0)
        dq_pieces = []
        dk_pieces = []
        dv_pieces = []
        for head_index in range(heads_here):
            low_col = head_index * HEAD_DIM
            high_col = low_col + HEAD_DIM
            query_head = query_block[:, low_col:high_col]
            key_head = keys_all[:, low_col:high_col]
            grad_head = grad_block[:, low_col:high_col]
            raw_scores = contract_cols(query_head, key_head)
            scores = jnp.where(visible, raw_scores * score_scale, MASKED_SCORE)
            soft_weights = jnp.exp(scores - logsum[head_index][:, None])
            d_soft = contract_cols(grad_head, values_all[:, low_col:high_col])
            d_scores = soft_weights * (
                d_soft - jnp.sum(soft_weights * d_soft, axis=1, keepdims=True)
            )
            d_raw = (d_scores * score_scale).astype(jnp.bfloat16)
            dq_pieces.append(jnp.dot(d_raw, key_head, preferred_element_type=jnp.float32))
            dk_pieces.append(contract_rows(d_raw, query_head))
            dv_pieces.append(contract_rows(soft_weights.astype(jnp.bfloat16), grad_head))
        new_carry = (
            d_keys_acc + jnp.concatenate(dk_pieces, axis=1),
            d_values_acc + jnp.concatenate(dv_pieces, axis=1),
        )
        return (new_carry, jnp.concatenate(dq_pieces, axis=1))

    zero_acc = jnp.zeros((seq_len, local_cols), jnp.float32)
    (d_keys, d_values), dq_blocks = lax.scan(
        backward_block, (zero_acc, zero_acc), (starts, logsum_blocks)
    )
    d_queries = dq_blocks.reshape(seq_len, local_cols)
    d_projected = jnp.stack([d_queries, d_keys, d_values], axis=1).astype(jnp.bfloat16)
    part_sums = jnp.sum(d_projected, axis=0, dtype=jnp.float32)
    d_qv_bias = lax.dynamic_update_slice(
        jnp.zeros((2, model_width), jnp.float32),
        jnp.stack([part_sums[0], part_sums[2]]),
        (0, tensor_pos * local_cols),
    )
    d_flat = d_projected.reshape(seq_len, 3 * local_cols)
    d_qkv_w = contract_rows(full_one, d_flat).reshape(model_width, 3, local_cols)
    d_normed_one = lax.psum_scatter(
        contract_cols(d_flat, qkv_flat_weight).astype(jnp.bfloat16),
        "tensor",
        scatter_dimension=0,
        tiled=True,
    ).astype(jnp.float32)
    unused_one, norm_back_one = jax.vjp(
        layer_norm, residual_in, gain_attn.astype(jnp.float32), offset_attn.astype(jnp.float32)
    )
    d_input_part, d_gain_attn, d_offset_attn = norm_back_one(d_normed_one)
    grad_tokens = (d_middle + d_input_part).astype(jnp.bfloat16)
    d_fc_bias_full = lax.dynamic_update_slice(
        jnp.zeros((fc_bias_all.shape[0],), jnp.float32), d_fc_bias, (tensor_pos * hidden_cols,)
    )
    (
        sum_gain_attn,
        sum_offset_attn,
        sum_qv_bias,
        sum_out_bias,
        sum_gain_mlp,
        sum_offset_mlp,
        sum_fc_bias,
        sum_proj_bias,
    ) = (
        lax.psum(d_gain_attn.astype(jnp.bfloat16), "tensor").astype(jnp.float32),
        lax.psum(d_offset_attn.astype(jnp.bfloat16), "tensor").astype(jnp.float32),
        lax.psum(d_qv_bias.astype(jnp.bfloat16), "tensor").astype(jnp.float32),
        lax.psum(d_out_bias.astype(jnp.bfloat16), "tensor").astype(jnp.float32),
        lax.psum(d_gain_mlp.astype(jnp.bfloat16), "tensor").astype(jnp.float32),
        lax.psum(d_offset_mlp.astype(jnp.bfloat16), "tensor").astype(jnp.float32),
        lax.psum(d_fc_bias_full.astype(jnp.bfloat16), "tensor").astype(jnp.float32),
        lax.psum(d_proj_bias.astype(jnp.bfloat16), "tensor").astype(jnp.float32),
    )
    (
        grad_w_qkv,
        grad_w_attn_out,
        grad_ln1_gain,
        grad_ln1_bias,
        grad_b_qv,
        grad_b_attn_out,
        grad_ln2_gain,
        grad_ln2_bias,
        grad_b_fc,
        grad_b_proj,
    ) = (
        lax.psum_scatter(d_qkv_w, "dp", scatter_dimension=0, tiled=True),
        lax.psum_scatter(d_out_w, "dp", scatter_dimension=1, tiled=True),
        lax.psum_scatter(sum_gain_attn, "dp", scatter_dimension=0, tiled=True),
        lax.psum_scatter(sum_offset_attn, "dp", scatter_dimension=0, tiled=True),
        lax.psum_scatter(sum_qv_bias, "dp", scatter_dimension=1, tiled=True),
        lax.psum_scatter(sum_out_bias, "dp", scatter_dimension=0, tiled=True),
        lax.psum_scatter(sum_gain_mlp, "dp", scatter_dimension=0, tiled=True),
        lax.psum_scatter(sum_offset_mlp, "dp", scatter_dimension=0, tiled=True),
        lax.psum_scatter(sum_fc_bias, "dp", scatter_dimension=0, tiled=True),
        lax.psum_scatter(sum_proj_bias, "dp", scatter_dimension=0, tiled=True),
    )
    return (
        block_out,
        grad_tokens,
        grad_ln1_gain,
        grad_ln1_bias,
        grad_w_qkv,
        grad_b_qv,
        grad_w_attn_out,
        grad_b_attn_out,
        grad_ln2_gain,
        grad_ln2_bias,
        grad_w_fc,
        grad_b_fc,
        grad_w_proj,
        grad_b_proj,
    )


def solution(mesh):
    in_specs = (
        P(("dp", "tensor"), None),
        P("dp", None),
        P("dp"),
        P("dp"),
        P("dp", None, "tensor"),
        P(None, "dp"),
        P("tensor", "dp"),
        P("dp"),
        P("dp"),
        P("dp"),
        P("dp", "tensor"),
        P("dp"),
        P("tensor", "dp"),
        P("dp"),
        P(("dp", "tensor"), None),
    )
    out_specs = (
        P(("dp", "tensor"), None),
        P(("dp", "tensor"), None),
        P("dp"),
        P("dp"),
        P("dp", None, "tensor"),
        P(None, "dp"),
        P("tensor", "dp"),
        P("dp"),
        P("dp"),
        P("dp"),
        P("dp", "tensor"),
        P("dp"),
        P("tensor", "dp"),
        P("dp"),
    )
    return jax.shard_map(
        on_device, mesh=mesh, in_specs=in_specs, out_specs=out_specs, check_vma=False
    )
```

profile of v0, /device:TPU:0, one launch (start us, length us, event | category | flops | bytes accessed | tf_op | source)
XLA Modules:
  0.0 1494.2 jit_solution(269349831955712147)
XLA Ops:
  16.5 63.2 %all-reduce.15 = (bf16[768]{0:T(1024)(128)(2,1)}, bf16[768]{0:T(1024)(128)(2,1)}, bf16[768]{0:T(1024)(128)(2,1)}, bf16[768]{0:T(1024)(128)(2,1)S(1)}, bf16[768]{...) all-reduce(bf16[768]{0:T(1024)(128)(2,1)S(1)} %dynamic-update-slice, ...), channel_id=1, replica_groups=mesh['dp'=16,'tensor'=2] {'dp'}, use_global_device_ids=true, to_apply=%add.4 | all-reduce | flops 7680 | bytes 30720
  86.6 17.0 %all-gather = bf16[16,48,2]{1,2,0:T(2,128)(2,1)S(1)} all-gather(bf16[1,48,2]{1,2,0:T(2,128)(2,1)S(1)} %bitcast.226), channel_id=1, replica_groups=mesh['dp'=16,'tensor'=2] {'dp'}, dimensions={0}, use_global_device_ids=true | all-gather | bytes 3264 | tf_op jit(solution)/shard_map/all_gather | solution.py:72
  104.4 22.1 %all_gather.60 = bf16[384,768]{0,1:T(8,128)(2,1)} all-gather(bf16[384,48]{0,1:T(8,128)(2,1)S(1)} %copy-done.41), channel_id=1, replica_groups=mesh['dp'=16,'tensor'=2] {'dp'}, dimensions={1}, use_global_device_ids=true | all-gather | bytes 626688 | tf_op jit(solution)/shard_map/all_gather | solution.py:73
  138.2 145.9 %while.43 = (s32[]{:T(128)}, bf16[4,512,384]{2,1,0:T(8,128)(2,1)}, f32[4,6,512]{2,1,0:T(8,128)}, s32[4]{0:T(128)}, s32[2048]{0:T(1024)}, /*index=5*/s32[1,2048]{...) while((s32[]{:T(128)}, bf16[4,512,384]{2,1,0:T(8,128)(2,1)}, ...), condition=%wide.region_15.16_spmd, body=%wide.region_2.15_spmd.sunk | while | flops 1680012800 | bytes 86346096 | solution.py:124
  293.8 39.7 %reduce-scatter.12.cloned.1.call-done = bf16[1024,768]{1,0:T(8,128)(2,1)} async-done(((bf16[2048,768]{1,0:T(8,128)(2,1)}), bf16[1024,768]{1,0:T(8,128)(2,1)}) %reduce-scatter.12.cloned.1.call-update) | async-done | bytes 1572880 | tf_op jit(solution)/shard_map/reduce_scatter | solution.py:126
  340.2 38.0 %all-gather.17.cloned.1.call-done = bf16[1536,768]{0,1:T(8,128)(2,1)} async-done(((bf16[1536,48]{0,1:T(8,128)(2,1)}), bf16[1536,768]{0,1:T(8,128)(2,1)}) %all-gather.17.cloned.1.call-update) | async-done | bytes 2359312 | tf_op jit(solution)/shard_map/all_gather | solution.py:142
  381.0 42.4 %all-gather.19.cloned.1.call-done = bf16[2048,768]{1,0:T(8,128)(2,1)} async-done(((bf16[1024,768]{1,0:T(8,128)(2,1)}), bf16[2048,768]{1,0:T(8,128)(2,1)}) %all-gather.19.cloned.1.call-update) | async-done | bytes 3145744 | tf_op jit(solution)/shard_map/all_gather | solution.py:191
  423.4 44.7 %all-gather.15.cloned.1.call-done = bf16[768,1536]{1,0:T(8,128)(2,1)} async-done(((bf16[48,1536]{1,0:T(8,128)(2,1)}), bf16[768,1536]{1,0:T(8,128)(2,1)}) %all-gather.15.cloned.1.call-update) | async-done | bytes 2359312 | tf_op jit(solution)/shard_map/all_gather | solution.py:140
  468.2 45.9 %all-gather.13.cloned.1.call-done = bf16[2048,768]{1,0:T(8,128)(2,1)} async-done(((bf16[1024,768]{1,0:T(8,128)(2,1)}), bf16[2048,768]{1,0:T(8,128)(2,1)}) %all-gather.13.cloned.1.call-update) | async-done | bytes 3145744 | tf_op jit(solution)/shard_map/all_gather | solution.py:151
  514.1 47.8 %while.44 = (s32[]{:T(128)}, bf16[2,1024,1536]{2,1,0:T(8,128)(2,1)}, bf16[2,1024,1536]{2,1,0:T(8,128)(2,1)}, f32[2,1536]{1,0:T(2,128)S(1)}, s32[2]{0:T(128)S(1)}...) while((s32[]{:T(128)}, ...), condition=%wide.region_22.23_spmd, body=%wide.region_20.22_spmd.sunk | while | flops 4882168320 | bytes 102281512 | solution.py:203
  562.0 9.1 convolution_convert_fusion.1
  572.7 14.0 convolution_convert_fusion.2
  586.8 27.8 %reduce-scatter.16.cloned.1.call-done = bf16[1024,768]{1,0:T(8,128)(2,1)} async-done(((bf16[2048,768]{1,0:T(8,128)(2,1)}), bf16[1024,768]{1,0:T(8,128)(2,1)}) %reduce-scatter.16.cloned.1.call-update) | async-done | bytes 1572880 | tf_op jit(solution)/shard_map/reduce_scatter | solution.py:215
  618.6 41.6 %reduce-scatter.14.cloned.1.call-done = bf16[1024,768]{1,0:T(8,128)(2,1)} async-done(((bf16[2048,768]{1,0:T(8,128)(2,1)}), bf16[1024,768]{1,0:T(8,128)(2,1)}) %reduce-scatter.14.cloned.1.call-update) | async-done | bytes 1572880 | tf_op jit(solution)/shard_map/reduce_scatter | solution.py:156
  668.3 45.0 %all-gather.21.cloned.1.call-done = bf16[2048,768]{1,0:T(8,128)(2,1)} async-done(((bf16[1024,768]{1,0:T(8,128)(2,1)}), bf16[2048,768]{1,0:T(8,128)(2,1)}) %all-gather.21.cloned.1.call-update) | async-done | bytes 3145744 | tf_op jit(solution)/shard_map/all_gather | solution.py:230
  718.2 344.7 %while.45 = (s32[]{:T(128)}, f32[2048,384]{0,1:T(8,128)}, f32[2048,384]{0,1:T(8,128)}, bf16[4,512,384]{2,1,0:T(8,128)(2,1)}, s32[4]{0:T(128)}, /*index=5*/s32[20...) while((s32[]{:T(128)}, f32[2048,384]{0,1:T(8,128)}, ...), condition=%wide.region_33.34_spmd.clone, body=%wide.region_26.33_spmd.clone.sunk | while | flops 4111463936 | bytes 254159472 | solution.py:267
  1079.4 41.8 %reduce-scatter.18.cloned.1.call-done = bf16[1024,768]{1,0:T(8,128)(2,1)} async-done(((bf16[2048,768]{1,0:T(8,128)(2,1)}), bf16[1024,768]{1,0:T(8,128)(2,1)}) %reduce-scatter.18.cloned.1.call-update) | async-done | bytes 1572880 | tf_op jit(solution)/shard_map/reduce_scatter | solution.py:280
  1138.5 10.1 fusion.173
  1150.5 9.5 fusion.172
  1183.0 60.1 %all-reduce.14 = (f32[768]{0:T(1024)S(1)}, f32[768]{0:T(1024)S(1)}, f32[768]{0:T(1024)S(1)}, f32[768]{0:T(1024)S(1)}, f32[768]{0:T(1024)S(1)}, /*index=5*/f32[3072]{0:T(1024)S(1)}, f32[768]{0:T(1024)S(1)}) all-reduce(bf16[768]{0:T(1024)(128)(2,1)S(1)} %get-tuple-element.392, ...), channel_id=6, replica_groups=mesh['dp'=16,'tensor'=2] {'dp'}, use_global_device_ids=true, to_apply=%region_39.40.clone | all-reduce | flops 7680 | bytes 46080
  1248.6 26.4 %reduce-scatter.26.cloned.1.call-done = f32[1536,48]{0,1:T(8,128)} async-done(((f32[1536,768]{0,1:T(8,128)}), f32[1536,48]{0,1:T(8,128)}) %reduce-scatter.26.cloned.1.call-update) | async-done | bytes 294928 | tf_op jit(solution)/shard_map/reduce_scatter | solution.py:213
  1275.1 78.9 %reduce-scatter.24.cloned.1.call-done = f32[48,1536]{1,0:T(8,128)} async-done(((f32[768,1536]{1,0:T(8,128)}), f32[48,1536]{1,0:T(8,128)}) %reduce-scatter.24.cloned.1.call-update) | async-done | bytes 294928 | tf_op jit(solution)/shard_map/reduce_scatter | solution.py:212
  1353.9 61.6 %reduce-scatter.22.cloned.1.call-done = f32[384,48]{0,1:T(8,128)} async-done(((f32[384,768]{0,1:T(8,128)}), f32[384,48]{0,1:T(8,128)}) %reduce-scatter.22.cloned.1.call-update) | async-done | bytes 73744 | tf_op jit(solution)/shard_map/reduce_scatter | solution.py:326
  1415.5 71.9 %reduce-scatter.20.cloned.1.call-done = f32[48,3,384]{2,0,1:T(8,128)} async-done(((f32[768,3,384]{2,0,1:T(8,128)}), f32[48,3,384]{2,0,1:T(8,128)}) %reduce-scatter.20.cloned.1.call-update) | async-done | bytes 221200 | tf_op jit(solution)/shard_map/reduce_scatter | solution.py:325
  (571 shorter events, 636.8 us)
Async XLA Ops:
  7.2 77.5 %copy-start = (bf16[1024,768]{1,0:T(8,128)(2,1)S(1)}, bf16[1024,768]{1,0:T(8,128)(2,1)}, u32[]{:S(2)}) copy-start(bf16[1024,768]{1,0:T(8,128)(2,1)} %param.21) | copy-start | bytes 4718596
  7.2 119.3 %all-gather.11.cloned.1.call-start = ((), (), s32[]{:S(2)}) async-start(), calls=%async_computation.10 | async-start | bytes 1880064 | tf_op jit(solution)/shard_map/all_gather | solution.py:71
  7.9 121.2 %all-gather.9.cloned.1.call-start = ((), (), s32[]{:S(2)}) async-start(), calls=%async_computation.9 | async-start | bytes 4718592 | tf_op jit(solution)/shard_map/all_gather | solution.py:85
  86.5 246.9 %reduce-scatter.12.cloned.1.call-start = ((), (), s32[]{:S(2)}) async-start(), calls=%async_computation.11 | async-start | bytes 4718592 | tf_op jit(solution)/shard_map/reduce_scatter | solution.py:126
  290.3 87.9 %all-gather.17.cloned.1.call-start = ((), (), s32[]{:S(2)}) async-start(), calls=%async_computation.14 | async-start | bytes 2506752 | tf_op jit(solution)/shard_map/all_gather | solution.py:142
  290.9 132.5 %all-gather.19.cloned.1.call-start = ((), (), s32[]{:S(2)}) async-start(), calls=%async_computation.16 | async-start | bytes 4718592 | tf_op jit(solution)/shard_map/all_gather | solution.py:191
  293.1 175.1 %all-gather.15.cloned.1.call-start = ((), (), s32[]{:S(2)}) async-start(), calls=%async_computation.13 | async-start | bytes 2506752 | tf_op jit(solution)/shard_map/all_gather | solution.py:140
  293.7 220.4 %all-gather.13.cloned.1.call-start = ((), (), s32[]{:S(2)}) async-start(), calls=%async_computation.12 | async-start | bytes 4718592 | tf_op jit(solution)/shard_map/all_gather | solution.py:151
  340.0 274.6 %reduce-scatter.16.cloned.1.call-start = ((), (), s32[]{:S(2)}) async-start(), calls=%async_computation.17 | async-start | bytes 4718592 | tf_op jit(solution)/shard_map/reduce_scatter | solution.py:215
  571.1 89.1 %reduce-scatter.14.cloned.1.call-start = ((), (), s32[]{:S(2)}) async-start(), calls=%async_computation.15 | async-start | bytes 4718592 | tf_op jit(solution)/shard_map/reduce_scatter | solution.py:156
  586.8 126.5 %all-gather.21.cloned.1.call-start = ((), (), s32[]{:S(2)}) async-start(), calls=%async_computation.18 | async-start | bytes 4718592 | tf_op jit(solution)/shard_map/all_gather | solution.py:230
  668.2 453.0 %reduce-scatter.18.cloned.1.call-start = ((), (), s32[]{:S(2)}) async-start(), calls=%async_computation.19 | async-start | bytes 4718592 | tf_op jit(solution)/shard_map/reduce_scatter | solution.py:280
  668.2 50.0 %copy-start.5 = (bf16[2048,384]{1,0:T(8,128)(2,1)S(1)}, bf16[2048,384]{1,0:T(8,128)(2,1)}, u32[]{:S(2)}) copy-start(bf16[2048,384]{1,0:T(8,128)(2,1)} %copy-done.4) | copy-start | bytes 4718596
  668.2 50.0 %copy-start.7 = (bf16[2048,384]{1,0:T(8,128)(2,1)S(1)}, bf16[2048,384]{1,0:T(8,128)(2,1)}, u32[]{:S(2)}) copy-start(bf16[2048,384]{1,0:T(8,128)(2,1)} %copy-done.6) | copy-start | bytes 4718596
  1077.7 43.5 %copy-start.3 = (bf16[1024,768]{1,0:T(8,128)(2,1)S(1)}, bf16[1024,768]{1,0:T(8,128)(2,1)}, u32[]{:S(2)}) copy-start(bf16[1024,768]{1,0:T(8,128)(2,1)} %param.21) | copy-start | bytes 4718596
  1077.7 43.5 %copy-start.22 = (f32[1024]{0:T(1024)S(1)}, f32[1024]{0:T(1024)}, u32[]{:S(2)}) copy-start(f32[1024]{0:T(1024)} %copy-done.21) | copy-start | bytes 12292
  1077.7 43.5 %copy-start.26 = (f32[768]{0:T(1024)S(1)}, f32[768]{0:T(1024)}, u32[]{:S(2)}) copy-start(f32[768]{0:T(1024)} %copy-done.25) | copy-start | bytes 9220
  1077.7 45.9 %copy-start.38 = (f32[1024]{0:T(1024)S(1)}, f32[1024]{0:T(1024)}, u32[]{:S(2)}) copy-start(f32[1024]{0:T(1024)} %copy-done.37) | copy-start | bytes 12292
  1077.7 45.9 %copy-start.30 = (f32[1024]{0:T(1024)S(1)}, f32[1024]{0:T(1024)}, u32[]{:S(2)}) copy-start(f32[1024]{0:T(1024)} %copy-done.29) | copy-start | bytes 12292
  1077.7 169.5 %reduce-scatter.28.cloned.1.call-start = ((), (), s32[]{:S(2)}) async-start(), calls=%async_computation.24 | async-start | bytes 417792
  1138.5 136.6 %reduce-scatter.26.cloned.1.call-start = ((), (), s32[]{:S(2)}) async-start(), calls=%async_computation.23 | async-start | bytes 5013504 | tf_op jit(solution)/shard_map/reduce_scatter | solution.py:213
  1148.6 205.3 %reduce-scatter.24.cloned.1.call-start = ((), (), s32[]{:S(2)}) async-start(), calls=%async_computation.22 | async-start | bytes 5013504 | tf_op jit(solution)/shard_map/reduce_scatter | solution.py:212
  1160.0 255.5 %reduce-scatter.22.cloned.1.call-start = ((), (), s32[]{:S(2)}) async-start(), calls=%async_computation.21 | async-start | bytes 1253376 | tf_op jit(solution)/shard_map/reduce_scatter | solution.py:326
  1166.3 321.1 %reduce-scatter.20.cloned.1.call-start = ((), (), s32[]{:S(2)}) async-start(), calls=%async_computation.20 | async-start | bytes 3760128 | tf_op jit(solution)/shard_map/reduce_scatter | solution.py:325
  (61 other events, 547.8 us)
Sparse Core Ops, SparseCore 0:
  10.3 43.2 all-gather.10
  86.6 42.1 all-gather.8
  290.4 43.0 reduce-scatter.11
  335.8 42.3 all-gather.16
  379.7 43.7 all-gather.18
  425.8 42.3 all-gather.14
  470.3 43.7 all-gather.12
  571.2 43.3 reduce-scatter.15
  616.8 43.3 reduce-scatter.13
  668.3 44.9 all-gather.20
  1077.8 43.3 reduce-scatter.17
  1138.6 56.7 reduce-scatter.27
  1200.3 74.7 reduce-scatter.25
  1279.4 74.5 reduce-scatter.23
  1358.4 57.0 reduce-scatter.21
  1420.3 67.0 reduce-scatter.19
where the time goes:
time: 1500 us; the launch traced here: 1490 us
  waiting for transfers between devices  608 us (41%)
  matrix products  437 us (29%)
  blocking collectives  169 us (11%)
  other arithmetic  126 us (8%)
  local copies, waits for them, and re-layouts  107 us (7%)
  loops' own time  29.1 us (2%)
  between operations  17.5 us (1%)
    dot_general x77, matrix products, contract_cols(): lax.dot_general(left, right, (((1,), (1,)), ((), ())), preferred_element_...  205 us
    dot_general x52, matrix products, contract_rows(): lax.dot_general(left, right, (((0,), (0,)), ((), ())), preferred_element_...  126 us
    unnamed x2, blocking collectives  123 us
    reduce_scatter x1, waiting for transfers between devices, on_device(): lax.psum_scatter(d_fc_w, 'dp', scatter_dimension=0, tiled=True)  78.9 us
    reduce_scatter x1, waiting for transfers between devices, on_device(): lax.psum_scatter(d_qkv_w, 'dp', scatter_dimension=0, tiled=True)  71.9 us
    reduce_scatter x1, waiting for transfers between devices, on_device(): lax.psum_scatter(d_out_w, 'dp', scatter_dimension=1, tiled=True)  61.6 us
    all_gather x1, waiting for transfers between devices, on_device(): full_two = lax.all_gather(normed_two, 'tensor', axis=0, tiled=True)  45.9 us
    all_gather x1, waiting for transfers between devices, on_device(): lax.all_gather(scaled_mid.astype(jnp.bfloat16), 'tensor', axis=0, tiled=T...  45 us
  transfers between devices with their start and end apart: 16, of which 13 were waited for; matrix products, arithmetic and copies ran while one was open for 6% of the time, Pallas kernels for 0%

commit v1 on v0

--- a/solution.py
+++ b/solution.py
@@ -56,6 +56,25 @@
     b_proj,
     cotangent,
 ):
+
+    def update_hubs(slab_in):
+        lower = lax.axis_size("dp")
+        y = lax.axis_index("dp")
+        copies = []
+        field_out, g_now, after = (lower, y, slab_in.shape[1])
+        for tick in range(field_out):
+            copies.append((tick, (tick + 1) % field_out))
+        response = slab_in
+        a_now = jnp.zeros(
+            (*slab_in.shape[:1], field_out * after, *slab_in.shape[2:]), slab_in.dtype
+        )
+        for d in range(field_out):
+            part_now = (g_now - d) % field_out
+            a_now = lax.dynamic_update_slice_in_dim(a_now, response, part_now * after, axis=1)
+            if d < field_out - 1:
+                response = lax.ppermute(response, "dp", copies)
+        return a_now
+
     model_width = tokens.shape[1]
     local_rows = tokens.shape[0]
     local_cols = w_qkv.shape[2]
@@ -139,7 +158,7 @@
         lax.all_gather(ln2_bias, "dp", axis=0, tiled=True),
         lax.all_gather(w_fc, "dp", axis=0, tiled=True),
         lax.all_gather(b_fc, "dp", axis=0, tiled=True),
-        lax.all_gather(w_proj, "dp", axis=1, tiled=True),
+        update_hubs(w_proj),
         lax.all_gather(b_proj, "dp", axis=0, tiled=True),
     )
     fc_bias = lax.dynamic_slice_in_dim(

time: 1500 us -> 1570 us (1.047)
  waiting for transfers between devices: 608 us -> 645 us
  loops' own time: 29.1 us -> 47.9 us
    ppermute x0 -> x15, waiting for transfers between devices: none -> 105 us  [update_hubs(): response = lax.ppermute(response, 'dp', copies)]
    all_gather x1, waiting for transfers between devices: 38 us -> 7.11 us  [on_device(): lax.all_gather(w_proj, 'dp', axis=1, tiled=True)]
    reduce_scatter x1, waiting for transfers between devices: 27.8 us -> 0.02 us  [on_device(): lax.psum_scatter(contract_cols(lax.slice_in_dim(d_pre_all, 0, lax.axis_si...]
    another operation x1, loops' own time: 16.5 us -> 35.3 us  [on_device(): lax.scan(backward_block, (zero_acc, zero_acc), (starts, logsum_blocks))]
  transfers between devices with their start and end apart: 16 -> 31, of which waited for: 13 -> 26; matrix products, arithmetic and copies ran while one was open for 6% -> 9% of each run, Pallas kernels for 0% -> 0%
where the time goes in v1:
time: 1570 us; the launch traced here: 1560 us
  waiting for transfers between devices  645 us (41%)
  matrix products  437 us (28%)
  blocking collectives  169 us (11%)
  other arithmetic  126 us (8%)
  local copies, waits for them, and re-layouts  112 us (7%)
  loops' own time  47.9 us (3%)
  between operations  18.1 us (1%)
    dot_general x77, matrix products, contract_cols(): lax.dot_general(left, right, (((1,), (1,)), ((), ())), preferred_element_...  205 us
    dot_general x52, matrix products, contract_rows(): lax.dot_general(left, right, (((0,), (0,)), ((), ())), preferred_element_...  126 us
    unnamed x2, blocking collectives  123 us
    ppermute x15, waiting for transfers between devices, update_hubs(): response = lax.ppermute(response, 'dp', copies)  105 us
    reduce_scatter x1, waiting for transfers between devices, on_device(): lax.psum_scatter(d_fc_w, 'dp', scatter_dimension=0, tiled=True)  79 us
    reduce_scatter x1, waiting for transfers between devices, on_device(): lax.psum_scatter(d_qkv_w, 'dp', scatter_dimension=0, tiled=True)  71.9 us
    reduce_scatter x1, waiting for transfers between devices, on_device(): lax.psum_scatter(d_out_w, 'dp', scatter_dimension=1, tiled=True)  61.6 us
    all_gather x1, waiting for transfers between devices, on_device(): full_two = lax.all_gather(normed_two, 'tensor', axis=0, tiled=True)  45.9 us
  transfers between devices with their start and end apart: 31, of which 26 were waited for; matrix products, arithmetic and copies ran while one was open for 9% of the time, Pallas kernels for 0%

profile of v1, /device:TPU:0, one launch (start us, length us, event | category | flops | bytes accessed | tf_op | source)
XLA Modules:
  0.0 1555.7 jit_solution(7905600409455726261)
XLA Ops:
  16.5 63.2 %all-reduce.15 = (bf16[768]{0:T(1024)(128)(2,1)}, bf16[768]{0:T(1024)(128)(2,1)}, bf16[768]{0:T(1024)(128)(2,1)}, bf16[768]{0:T(1024)(128)(2,1)S(1)}, bf16[768]{...) all-reduce(bf16[768]{0:T(1024)(128)(2,1)S(1)} %dynamic-update-slice, ...), channel_id=1, replica_groups=mesh['dp'=16,'tensor'=2] {'dp'}, use_global_device_ids=true, to_apply=%add.4 | all-reduce | flops 7680 | bytes 30720
  86.6 17.0 %all-gather = bf16[16,48,2]{1,2,0:T(2,128)(2,1)S(1)} all-gather(bf16[1,48,2]{1,2,0:T(2,128)(2,1)S(1)} %bitcast.226), channel_id=1, replica_groups=mesh['dp'=16,'tensor'=2] {'dp'}, dimensions={0}, use_global_device_ids=true | all-gather | bytes 3264 | tf_op jit(solution)/shard_map/all_gather | solution.py:91
  104.4 22.1 %all_gather.59 = bf16[384,768]{0,1:T(8,128)(2,1)} all-gather(bf16[384,48]{0,1:T(8,128)(2,1)S(1)} %copy-done.44), channel_id=1, replica_groups=mesh['dp'=16,'tensor'=2] {'dp'}, dimensions={1}, use_global_device_ids=true | all-gather | bytes 626688 | tf_op jit(solution)/shard_map/all_gather | solution.py:92
  138.1 145.7 %while.43 = (s32[]{:T(128)}, bf16[4,512,384]{2,1,0:T(8,128)(2,1)}, f32[4,6,512]{2,1,0:T(8,128)}, s32[4]{0:T(128)}, s32[2048]{0:T(1024)}, /*index=5*/s32[1,2048]{...) while((s32[]{:T(128)}, bf16[4,512,384]{2,1,0:T(8,128)(2,1)}, ...), condition=%wide.region_15.16_spmd, body=%wide.region_2.15_spmd.sunk | while | flops 1680012800 | bytes 86346096 | solution.py:143
  293.6 39.6 %reduce-scatter.12.cloned.1.call-done = bf16[1024,768]{1,0:T(8,128)(2,1)} async-done(((bf16[2048,768]{1,0:T(8,128)(2,1)}), bf16[1024,768]{1,0:T(8,128)(2,1)}) %reduce-scatter.12.cloned.1.call-update) | async-done | bytes 1572880 | tf_op jit(solution)/shard_map/reduce_scatter | solution.py:145
  346.7 8.7 collective-permute-done.1
  362.6 10.4 collective-permute-done.3
  384.4 41.2 %all-gather.17.cloned.1.call-done = bf16[2048,768]{1,0:T(8,128)(2,1)} async-done(((bf16[1024,768]{1,0:T(8,128)(2,1)}), bf16[2048,768]{1,0:T(8,128)(2,1)}) %all-gather.17.cloned.1.call-update) | async-done | bytes 3145744 | tf_op jit(solution)/shard_map/all_gather | solution.py:210
  425.6 44.7 %all-gather.15.cloned.1.call-done = bf16[768,1536]{1,0:T(8,128)(2,1)} async-done(((bf16[48,1536]{1,0:T(8,128)(2,1)}), bf16[768,1536]{1,0:T(8,128)(2,1)}) %all-gather.15.cloned.1.call-update) | async-done | bytes 2359312 | tf_op jit(solution)/shard_map/all_gather | solution.py:159
  470.4 45.9 %all-gather.13.cloned.1.call-done = bf16[2048,768]{1,0:T(8,128)(2,1)} async-done(((bf16[1024,768]{1,0:T(8,128)(2,1)}), bf16[2048,768]{1,0:T(8,128)(2,1)}) %all-gather.13.cloned.1.call-update) | async-done | bytes 3145744 | tf_op jit(solution)/shard_map/all_gather | solution.py:170
  516.3 47.9 %while.44 = (s32[]{:T(128)}, bf16[2,1024,1536]{2,1,0:T(8,128)(2,1)}, bf16[2,1024,1536]{2,1,0:T(8,128)(2,1)}, f32[2,1536]{1,0:T(2,128)S(1)}, s32[2]{0:T(128)S(1)}...) while((s32[]{:T(128)}, ...), condition=%wide.region_22.23_spmd, body=%wide.region_20.22_spmd.sunk | while | flops 4882168320 | bytes 111718728 | solution.py:222
  564.3 9.0 convolution_convert_fusion.1
  648.9 14.2 convolution_convert_fusion.2
  668.9 33.7 %reduce-scatter.14.cloned.1.call-done = bf16[1024,768]{1,0:T(8,128)(2,1)} async-done(((bf16[2048,768]{1,0:T(8,128)(2,1)}), bf16[1024,768]{1,0:T(8,128)(2,1)}) %reduce-scatter.14.cloned.1.call-update) | async-done | bytes 1572880 | tf_op jit(solution)/shard_map/reduce_scatter | solution.py:175
  710.7 45.0 %all-gather.21.cloned.1.call-done = bf16[2048,768]{1,0:T(8,128)(2,1)} async-done(((bf16[1024,768]{1,0:T(8,128)(2,1)}), bf16[2048,768]{1,0:T(8,128)(2,1)}) %all-gather.21.cloned.1.call-update) | async-done | bytes 3145744 | tf_op jit(solution)/shard_map/all_gather | solution.py:249
  760.7 363.6 %while.45 = (s32[]{:T(128)}, f32[2048,384]{0,1:T(8,128)}, f32[2048,384]{0,1:T(8,128)}, bf16[4,512,384]{2,1,0:T(8,128)(2,1)}, s32[4]{0:T(128)}, /*index=5*/s32[20...) while((s32[]{:T(128)}, f32[2048,384]{0,1:T(8,128)}, ...), condition=%wide.region_33.34_spmd.clone, body=%wide.region_26.33_spmd.clone.sunk | while | flops 4111463936 | bytes 254159472 | solution.py:286
  1140.8 41.8 %reduce-scatter.18.cloned.1.call-done = bf16[1024,768]{1,0:T(8,128)(2,1)} async-done(((bf16[2048,768]{1,0:T(8,128)(2,1)}), bf16[1024,768]{1,0:T(8,128)(2,1)}) %reduce-scatter.18.cloned.1.call-update) | async-done | bytes 1572880 | tf_op jit(solution)/shard_map/reduce_scatter | solution.py:299
  1199.9 10.0 fusion.173
  1211.9 9.6 fusion.172
  1244.4 60.0 %all-reduce.14 = (f32[768]{0:T(1024)S(1)}, f32[768]{0:T(1024)S(1)}, f32[768]{0:T(1024)S(1)}, f32[768]{0:T(1024)S(1)}, f32[768]{0:T(1024)S(1)}, /*index=5*/f32[3072]{0:T(1024)S(1)}, f32[768]{0:T(1024)S(1)}) all-reduce(bf16[768]{0:T(1024)(128)(2,1)S(1)} %get-tuple-element.392, ...), channel_id=6, replica_groups=mesh['dp'=16,'tensor'=2] {'dp'}, use_global_device_ids=true, to_apply=%region_39.40.clone | all-reduce | flops 7680 | bytes 46080
  1310.0 26.5 %reduce-scatter.26.cloned.1.call-done = f32[1536,48]{0,1:T(8,128)} async-done(((f32[1536,768]{0,1:T(8,128)}), f32[1536,48]{0,1:T(8,128)}) %reduce-scatter.26.cloned.1.call-update) | async-done | bytes 294928 | tf_op jit(solution)/shard_map/reduce_scatter | solution.py:232
  1336.5 79.0 %reduce-scatter.24.cloned.1.call-done = f32[48,1536]{1,0:T(8,128)} async-done(((f32[768,1536]{1,0:T(8,128)}), f32[48,1536]{1,0:T(8,128)}) %reduce-scatter.24.cloned.1.call-update) | async-done | bytes 294928 | tf_op jit(solution)/shard_map/reduce_scatter | solution.py:231
  1415.4 61.6 %reduce-scatter.22.cloned.1.call-done = f32[384,48]{0,1:T(8,128)} async-done(((f32[384,768]{0,1:T(8,128)}), f32[384,48]{0,1:T(8,128)}) %reduce-scatter.22.cloned.1.call-update) | async-done | bytes 73744 | tf_op jit(solution)/shard_map/reduce_scatter | solution.py:345
  1477.1 71.9 %reduce-scatter.20.cloned.1.call-done = f32[48,3,384]{2,0,1:T(8,128)} async-done(((f32[768,3,384]{2,0,1:T(8,128)}), f32[48,3,384]{2,0,1:T(8,128)}) %reduce-scatter.20.cloned.1.call-update) | async-done | bytes 221200 | tf_op jit(solution)/shard_map/reduce_scatter | solution.py:344
  (626 shorter events, 734.5 us)
Async XLA Ops:
  7.2 119.3 %all-gather.11.cloned.1.call-start = ((), (), s32[]{:S(2)}) async-start(), calls=%async_computation.10 | async-start | bytes 1880064 | tf_op jit(solution)/shard_map/all_gather | solution.py:90
  7.9 121.2 %all-gather.9.cloned.1.call-start = ((), (), s32[]{:S(2)}) async-start(), calls=%async_computation.9 | async-start | bytes 4718592 | tf_op jit(solution)/shard_map/all_gather | solution.py:104
  86.5 246.7 %reduce-scatter.12.cloned.1.call-start = ((), (), s32[]{:S(2)}) async-start(), calls=%async_computation.11 | async-start | bytes 4718592 | tf_op jit(solution)/shard_map/reduce_scatter | solution.py:145
  290.0 90.1 %all-gather.19.cloned.1.call-start = ((), (), s32[]{:S(2)}) async-start(), calls=%async_computation.16 | async-start | bytes 2506752 | tf_op jit(solution)/shard_map/all_gather | solution.py:201
  290.6 135.0 %all-gather.17.cloned.1.call-start = ((), (), s32[]{:S(2)}) async-start(), calls=%async_computation.15 | async-start | bytes 4718592 | tf_op jit(solution)/shard_map/all_gather | solution.py:210
  292.9 177.5 %all-gather.15.cloned.1.call-start = ((), (), s32[]{:S(2)}) async-start(), calls=%async_computation.13 | async-start | bytes 2506752 | tf_op jit(solution)/shard_map/all_gather | solution.py:159
  293.4 222.9 %all-gather.13.cloned.1.call-start = ((), (), s32[]{:S(2)}) async-start(), calls=%async_computation.12 | async-start | bytes 4718592 | tf_op jit(solution)/shard_map/all_gather | solution.py:170
  339.2 324.0 %reduce-scatter.16.cloned.1.call-start = ((), (), s32[]{:S(2)}) async-start(), calls=%async_computation.17 | async-start | bytes 4718592 | tf_op jit(solution)/shard_map/reduce_scatter | solution.py:234
  339.3 7.4 collective-permute-start
  346.6 8.7 collective-permute-start.1
  355.3 7.3 collective-permute-start.2
  362.6 10.4 collective-permute-start.3
  373.0 202.9 %collective-permute-start.4 = (bf16[1536,48]{0,1:T(8,128)(2,1)}, bf16[1536,48]{0,1:T(8,128)(2,1)}, u32[]{:S(2)}, u32[]{:S(2)}) collective-permute-start(bf16[1536,48]{0,1:T(8,128)(2,1)} %collective-permute-done.3), channel_id=1, source_target_pairs={{0,2},{2,4},{4,6},{6,8},{8,10},{10,12},{12,14},{14,16},{16,18},{18... | collective-permute-start | bytes 442376 | tf_op jit(solution)/shard_map/ppermute | solution.py:75
  573.3 129.4 %reduce-scatter.14.cloned.1.call-start = ((), (), s32[]{:S(2)}) async-start(), calls=%async_computation.14 | async-start | bytes 4718592 | tf_op jit(solution)/shard_map/reduce_scatter | solution.py:175
  575.9 7.5 collective-permute-start.5
  583.4 7.3 collective-permute-start.6
  590.7 7.3 collective-permute-start.7
  663.1 92.6 %all-gather.21.cloned.1.call-start = ((), (), s32[]{:S(2)}) async-start(), calls=%async_computation.18 | async-start | bytes 4718592 | tf_op jit(solution)/shard_map/all_gather | solution.py:249
  710.6 471.9 %reduce-scatter.18.cloned.1.call-start = ((), (), s32[]{:S(2)}) async-start(), calls=%async_computation.19 | async-start | bytes 4718592 | tf_op jit(solution)/shard_map/reduce_scatter | solution.py:299
  1139.1 169.5 %reduce-scatter.28.cloned.1.call-start = ((), (), s32[]{:S(2)}) async-start(), calls=%async_computation.24 | async-start | bytes 417792
  1199.9 136.6 %reduce-scatter.26.cloned.1.call-start = ((), (), s32[]{:S(2)}) async-start(), calls=%async_computation.23 | async-start | bytes 5013504 | tf_op jit(solution)/shard_map/reduce_scatter | solution.py:232
  1210.0 205.5 %reduce-scatter.24.cloned.1.call-start = ((), (), s32[]{:S(2)}) async-start(), calls=%async_computation.22 | async-start | bytes 5013504 | tf_op jit(solution)/shard_map/reduce_scatter | solution.py:231
  1221.4 255.7 %reduce-scatter.22.cloned.1.call-start = ((), (), s32[]{:S(2)}) async-start(), calls=%async_computation.21 | async-start | bytes 1253376 | tf_op jit(solution)/shard_map/reduce_scatter | solution.py:345
  1227.7 321.3 %reduce-scatter.20.cloned.1.call-start = ((), (), s32[]{:S(2)}) async-start(), calls=%async_computation.20 | async-start | bytes 3760128 | tf_op jit(solution)/shard_map/reduce_scatter | solution.py:344
  (80 other events, 986.8 us)
Sparse Core Ops, SparseCore 0:
  10.3 43.2 all-gather.10
  86.6 42.1 all-gather.8
  290.1 43.0 reduce-scatter.11
  335.6 44.4 all-gather.18
  381.6 44.0 all-gather.16
  428.0 42.3 all-gather.14
  472.6 43.7 all-gather.12
  573.4 43.3 reduce-scatter.15
  663.2 39.4 reduce-scatter.13
  710.7 44.9 all-gather.20
  1139.2 43.3 reduce-scatter.17
  1200.0 56.7 reduce-scatter.27
  1261.7 74.7 reduce-scatter.25
  1340.8 74.6 reduce-scatter.23
  1419.9 57.1 reduce-scatter.21
  1481.9 67.0 reduce-scatter.19
